TPU v7x, 32 devices: a whole 2x2x4 slice. The times are simulated.
32 devices in a mesh: sp: 4 (over y, x), ep: 8 (over z, core).
Axes of the slice: x: 2, y: 2, z: 4, core: 2. Of those that a mesh axis runs over, the one named last changes fastest.
Arguments:
- residual: bfloat16 [4096, 4096], P(('sp', 'ep')), may hold values from -40 to 40
- queries: bfloat16 [4096, 4096], P(('sp', 'ep')), may hold values from -6 to 6
- key_rows: bfloat16 [4096, 1024], P(('sp', 'ep')), may hold values from -6 to 6
- value_rows: bfloat16 [4096, 1024], P(('sp', 'ep')), may hold values from -6 to 6
- visible: int32 [32, 5], replicated, may hold values from 0 to 1, as said below
- out_proj: bfloat16 [4096, 4096], P(('sp', 'ep')), may hold values from -0.09375 to 0.09375
- norm_gain: float32 [4096], replicated, may hold values from 0.5 to 1.5
- expert_ids: int32 [4096, 2], P(('sp', 'ep')), may hold values from 0 to 7, all different within a row; in each aligned block of 128 rows (0 to 127, 128 to 255, ...) at most 40 rows name the same one
- route_weight: float32 [4096, 2], P(('sp', 'ep')), may hold values from 0.2 to 1
- expert_gate: bfloat16 [2, 7168, 4096], P(None, 'ep'), may hold values from -0.09375 to 0.09375
- expert_up: bfloat16 [2, 7168, 4096], P(None, 'ep'), may hold values from -0.09375 to 0.09375
- expert_down: bfloat16 [2, 7168, 4096], P(None, 'ep'), may hold values from -0.0625 to 0.0625
Outputs:
- layer_out: bfloat16 [4096, 4096], P(('sp', 'ep'))
Inputs may be any that keep to these rules, and one draw needn't show every extreme that they name: The sequence is packed with documents that are runs of whole blocks of 128 tokens, the first of them 5 blocks or longer; visible[q, d] is 1 exactly when block q - d exists and lies in the document of block q, so visible[q, 0] = 1. `expert_ids`: each token names two different experts. Among the 128 tokens of one block no expert is named by more than 40 tokens.
All inputs are finite; a program needn't handle non-finite values.
Results may differ from a plain program's by a relative error of at most 0.0065.
Values may be sent and summed in bfloat16 or wider, within the bound.
A program may use at most 128 MiB of HBM per device.

v0:
```python
import math
import jax
import jax.numpy as jnp
from jax import lax
from jax.sharding import PartitionSpec as P

HEAD = 128
CAP = 40


def settle(shard_piece, distance, ep_index):
    lowered = jnp.concatenate([jnp.zeros_like(shard_piece[:1]), shard_piece[:-1]], axis=0)
    return jnp.where(distance > ep_index, lowered, shard_piece)


def local(
    residual,
    queries,
    key_rows,
    value_rows,
    visible,
    out_proj,
    norm_gain,
    expert_ids,
    route_weight,
    expert_gate,
    expert_up,
    expert_down,
):
    sp_count = lax.axis_size("sp")
    ep_count = lax.axis_size("ep")
    ep_index = lax.axis_index("ep")
    tokens = residual.shape[0]
    reach = ep_count // 2 + 1
    query_width = queries.shape[1] // sp_count
    key_width = key_rows.shape[1] // sp_count
    key_heads = key_width // HEAD
    grouping = query_width // key_width
    query_send = queries.reshape(1, tokens, sp_count, query_width)
    key_send = key_rows.reshape(1, tokens, sp_count, key_width)
    value_send = value_rows.reshape(1, tokens, sp_count, key_width)
    query_heads, key_local, value_local = (
        lax.all_to_all(query_send, "sp", split_axis=2, concat_axis=0, tiled=True),
        lax.all_to_all(key_send, "sp", split_axis=2, concat_axis=0, tiled=True),
        lax.all_to_all(value_send, "sp", split_axis=2, concat_axis=0, tiled=True),
    )
    key_value = jnp.concatenate(
        [
            key_local.reshape(sp_count, tokens, key_width),
            value_local.reshape(sp_count, tokens, key_width),
        ],
        axis=2,
    )
    pieces = [key_value]
    gathered = lax.all_gather(key_value[None], "ep", axis=0, tiled=True)
    for distance in range(1, reach):
        source = (ep_index - distance) % ep_count
        pieces.append(
            settle(
                lax.dynamic_index_in_dim(gathered, source, 0, keepdims=False), distance, ep_index
            )
        )
    window = jnp.stack(pieces, axis=0)
    key_window = window[..., :key_width].reshape(reach, sp_count, tokens, key_heads, HEAD)
    value_window = window[..., key_width:].reshape(reach, sp_count, tokens, key_heads, HEAD)
    query_local = query_heads.reshape(sp_count, tokens, key_heads, grouping, HEAD)
    scores = jnp.einsum(
        "stgrh,dsugh->sgrtdu", query_local, key_window, preferred_element_type=jnp.float32
    ) * (1.0 / math.sqrt(HEAD))
    seen = lax.dynamic_index_in_dim(
        visible.reshape(sp_count, ep_count, reach), ep_index, 1, keepdims=False
    )
    position = jnp.arange(tokens)
    distances = jnp.arange(reach)
    allowed = (seen[:, None, :, None] > 0) & (
        (distances[None, None, :, None] > 0)
        | (position[None, None, None, :] <= position[None, :, None, None])
    )
    allowed = allowed[:, None, None]
    scores = jnp.where(allowed, scores, -1e30)
    peak = jnp.max(scores, axis=(4, 5), keepdims=True)
    weights_f = jnp.where(allowed, jnp.exp(scores - peak), 0.0)
    totals = jnp.sum(weights_f, axis=(4, 5))
    weights_b = weights_f.astype(jnp.bfloat16)
    summed = jnp.einsum(
        "sgrtdu,dsugh->stgrh", weights_b, value_window, preferred_element_type=jnp.float32
    )
    attended = (summed / jnp.transpose(totals, (0, 3, 1, 2))[..., None]).astype(jnp.bfloat16)
    attended = attended.reshape(sp_count * tokens, query_width)
    proj_full = lax.all_gather(out_proj, "ep", axis=0, tiled=True)
    projected = lax.psum_scatter(
        jnp.dot(attended, proj_full, preferred_element_type=jnp.float32).astype(jnp.bfloat16),
        "sp",
        scatter_dimension=0,
        tiled=True,
    ).astype(jnp.float32)
    hidden_sum = residual.astype(jnp.float32) + projected
    mean_square = jnp.mean(hidden_sum * hidden_sum, axis=-1, keepdims=True)
    normed = (hidden_sum * lax.rsqrt(mean_square + 1e-05) * norm_gain).astype(jnp.bfloat16)
    window_experts = expert_gate.shape[0]
    capacity = CAP
    choose = expert_ids[None] == jnp.arange(window_experts, dtype=jnp.int32)[:, None, None]
    member = jnp.any(choose, axis=2)
    token_weight = jnp.sum(jnp.where(choose, route_weight[None], 0.0), axis=2)
    ranked = jnp.cumsum(member.astype(jnp.int32), axis=1) - member.astype(jnp.int32)
    slot_hit = (
        ranked[:, None, :] == jnp.arange(capacity, dtype=jnp.int32)[None, :, None]
    ) & member[:, None, :]
    dispatch = slot_hit.astype(jnp.bfloat16)
    outgoing = jnp.einsum(
        "wct,td->wcd", dispatch, normed, preferred_element_type=jnp.float32
    ).astype(jnp.bfloat16)
    combine = jnp.where(slot_hit, token_weight[:, None, :], 0.0)
    shard_piece = lax.all_gather(outgoing, "ep", axis=1, tiled=True)
    gate_act = jnp.einsum(
        "wnd,wfd->wnf", shard_piece, expert_gate, preferred_element_type=jnp.float32
    )
    up_act = jnp.einsum("wnd,wfd->wnf", shard_piece, expert_up, preferred_element_type=jnp.float32)
    activated = (jax.nn.silu(gate_act) * up_act).astype(jnp.bfloat16)
    partial_value = jnp.einsum(
        "wnf,wfd->wnd", activated, expert_down, preferred_element_type=jnp.float32
    )
    returned = lax.psum_scatter(
        partial_value.astype(jnp.bfloat16), "ep", scatter_dimension=1, tiled=True
    ).astype(jnp.float32)
    expert_mix = jnp.einsum("wct,wcd->td", combine, returned, precision=lax.Precision.HIGHEST)
    return (hidden_sum + expert_mix).astype(jnp.bfloat16)


def solution(mesh):
    return jax.shard_map(
        local,
        mesh=mesh,
        in_specs=(
            P(("sp", "ep"), None),
            P(("sp", "ep"), None),
            P(("sp", "ep"), None),
            P(("sp", "ep"), None),
            P(),
            P(("sp", "ep"), None),
            P(),
            P(("sp", "ep"), None),
            P(("sp", "ep"), None),
            P(None, "ep", None),
            P(None, "ep", None),
            P(None, "ep", None),
        ),
        out_specs=P(("sp", "ep"), None),
        check_vma=False,
    )
```

profile of v0, /device:TPU:0, one launch (start us, length us, event | category | flops | bytes accessed | tf_op | source)
XLA Modules:
  0.0 411.7 jit_solution(12363634068117116235)
XLA Ops:
  6.5 1.8 copy.45
  8.3 5.3 %all-to-all-start = ((bf16[1,128,4,256]{1,3,0,2:T(8,128)(2,1)}), bf16[1,128,4,256]{1,3,0,2:T(8,128)(2,1)S(1)}, u32[]{:S(2)}, u32[]{:S(2)}) async-start(bf16[1,128,4,256]{1,3,0,2:T(8,128)(2,1)} %bitcast), calls=%async_computation | async-start | bytes 524288 | tf_op jit(solution)/shard_map/all_to_all | solution.py:44
  14.8 4.2 %all-to-all-done = bf16[1,128,4,256]{1,3,0,2:T(8,128)(2,1)S(1)} async-done(((bf16[1,128,4,256]{1,3,0,2:T(8,128)(2,1)}), bf16[1,128,4,256]{1,3,0,2:T(8,128)(2,1)S(1)}, u32[]{:S(2)}, u32[]{:S(2)}) %all-to-all-start) | async-done | bytes 262176 | tf_op jit(solution)/shard_map/all_to_all | solution.py:44
  19.0 8.1 %all_to_all.45 = bf16[1,128,4,256]{1,3,0,2:T(8,128)(2,1)S(1)} all-to-all(bf16[1,128,4,256]{1,3,0,2:T(8,128)(2,1)S(1)} %bitcast.130), channel_id=1, replica_groups=mesh['sp'=4,'ep'=8] {'sp'}, dimensions={2} | all-to-all | bytes 524288 | tf_op jit(solution)/shard_map/all_to_all | solution.py:45
  30.3 3.5 all-to-all-start.2
  36.2 38.7 %all-gather.9.cloned.1.call-done = bf16[32,128,512]{2,1,0:T(8,128)(2,1)} async-done(((bf16[4,128,512]{2,1,0:T(8,128)(2,1)}), bf16[32,128,512]{2,1,0:T(8,128)(2,1)}) %all-gather.9.cloned.1.call-update) | async-done | bytes 4194320 | tf_op jit(solution)/shard_map/all_gather | solution.py:55
  75.0 6.4 %copy.48 = bf16[32,128,512]{1,2,0:T(8,128)(2,1)} copy(bf16[32,128,512]{2,1,0:T(8,128)(2,1)} %all-gather.9.cloned.1.call-done) | data formatting | bytes 8388608 | tf_op jit(solution)/shard_map/all_gather | solution.py:55
  81.4 1.7 dynamic-slice_bitcast_fusion
  90.3 2.7 fusion
  93.0 6.6 %fusion.1 = (f32[4,2,4,128]{3,2,1,0:T(4,128)S(1)}, bf16[4,2,4,128,5,128]{3,5,2,4,1,0:T(8,128)(2,1)}) fusion(f32[4,2,5,128,128,4]{4,3,5,2,1,0:T(8,128)S(1)} %get-tuple-element.14, f32[4,2,4,128]{3,2,1,0:T(4,128)S(1)} %get-tuple-element.13, pred[4,128,5,128]{1,3,2,0:T(8,128)(4,1)} %broadcast_and_fusion), kind=kLoop, calls=%fused_computation.3 | loop fusion | flops 15724544 | bytes 16089088 | tf_op jit(solution)/shard_map/reduce_sum | solution.py:83
  99.6 3.5 fusion.7
  104.7 52.8 %all-gather.5.cloned.1.call-done = bf16[1024,4096]{1,0:T(8,128)(2,1)} async-done(((bf16[128,4096]{1,0:T(8,128)(2,1)}), bf16[1024,4096]{1,0:T(8,128)(2,1)}) %all-gather.5.cloned.1.call-update) | async-done | bytes 8388624 | tf_op jit(solution)/shard_map/all_gather | solution.py:90
  157.4 9.4 %convolution_convert_fusion.1 = bf16[512,4096]{1,0:T(8,128)(2,1)} fusion(bf16[512,1024]{1,0:T(8,128)(2,1)S(1)} %reshape.110, bf16[1024,4096]{1,0:T(8,128)(2,1)} %all-gather.5.cloned.1.call-done), kind=kOutput, calls=%fused_computation.6 | convolution fusion | flops 4297064448 | bytes 13631488 | tf_op jit(solution)/shard_map/dot_general | solution.py:92
  167.8 50.3 %reduce-scatter.5.cloned.1.call-done = bf16[128,4096]{1,0:T(8,128)(2,1)} async-done(((bf16[512,4096]{1,0:T(8,128)(2,1)}), bf16[128,4096]{1,0:T(8,128)(2,1)}) %reduce-scatter.5.cloned.1.call-update) | async-done | bytes 1048592 | tf_op jit(solution)/shard_map/reduce_scatter | solution.py:91
  218.1 1.6 multiply_reduce_fusion
  219.8 2.7 convolution_convert_fusion.2
  222.5 56.1 %all-gather.7.cloned.1.call-done = bf16[2,320,4096]{2,1,0:T(8,128)(2,1)} async-done(((bf16[2,40,4096]{2,1,0:T(8,128)(2,1)}), bf16[2,320,4096]{2,1,0:T(8,128)(2,1)}) %all-gather.7.cloned.1.call-update) | async-done | bytes 5242896 | tf_op jit(solution)/shard_map/all_gather | solution.py:114
  278.6 16.7 %fusion.31 = f32[2,320,896]{2,1,0:T(8,128)} fusion(bf16[2,320,4096]{2,1,0:T(8,128)(2,1)} %all-gather.7.cloned.1.call-done, bf16[2,896,4096]{2,1,0:T(8,128)(2,1)} %param.21), kind=kOutput, calls=%fused_computation.62 | convolution fusion | flops 4697620480 | bytes 22216704 | tf_op jit(solution)/shard_map/wnd,wfd->wnf/dot_general | solution.py:115
  295.3 25.4 %convolution_convert_fusion = bf16[2,320,4096]{2,1,0:T(8,128)(2,1)} fusion(bf16[2,896,4096]{2,1,0:T(8,128)(2,1)} %param.23, f32[2,320,896]{2,1,0:T(8,128)} %fusion.31, bf16[2,320,4096]{2,1,0:T(8,128)(2,1)} %all-gather.7.cloned.1.call-done, bf16[2,896,4096]{2,1,0:T(8,128)(2,1)} %param.22), kind=kOutput, calls=%fused_computation.5 | convolution fusion | flops 9401303040 | bytes 42139648 | tf_op jit(solution)/shard_map/wnf,wfd->wnd/dot_general | solution.py:120
  320.7 10.3 %copy.68 = bf16[2,320,4096]{2,0,1:T(2,128)(2,1)} copy(bf16[2,320,4096]{2,1,0:T(8,128)(2,1)} %convolution_convert_fusion) | data formatting | bytes 10485760
  331.1 10.7 %copy.71 = bf16[40,8,2,4096]{3,1,2,0:T(8,128)(2,1)} copy(bf16[40,8,2,4096]{3,2,1,0:T(2,128)(2,1)} %bitcast.116) | data formatting | bytes 10485760
  342.5 58.1 %reduce-scatter.7.cloned.1.call-done = bf16[40,8192]{1,0:T(8,128)(2,1)} async-done(((bf16[320,8192]{1,0:T(8,128)(2,1)}), bf16[40,8192]{1,0:T(8,128)(2,1)}) %reduce-scatter.7.cloned.1.call-update) | async-done | bytes 655376
  400.6 2.3 reshape.119
  402.9 2.2 fusion.6
  (55 shorter events, 16.9 us)
Async XLA Ops:
  8.3 20.7 %copy-start.4 = (bf16[128,4096]{1,0:T(8,128)(2,1)S(1)}, bf16[128,4096]{1,0:T(8,128)(2,1)}, u32[]{:S(2)}) copy-start(bf16[128,4096]{1,0:T(8,128)(2,1)} %param.13) | copy-start | bytes 3145732
  8.3 10.7 %all-to-all-start = ((bf16[1,128,4,256]{1,3,0,2:T(8,128)(2,1)}), bf16[1,128,4,256]{1,3,0,2:T(8,128)(2,1)S(1)}, u32[]{:S(2)}, u32[]{:S(2)}) async-start(bf16[1,128,4,256]{1,3,0,2:T(8,128)(2,1)} %bitcast), calls=%async_computation | async-start | bytes 524288 | tf_op jit(solution)/shard_map/all_to_all | solution.py:44
  13.7 61.3 %all-gather.9.cloned.1.call-start = ((), (), s32[]{:S(2)}) async-start(), calls=%async_computation.8 | async-start | bytes 4718592 | tf_op jit(solution)/shard_map/all_gather | solution.py:55
  28.2 5.8 %copy-start.6 = (s32[32,5]{0,1:T(8,128)S(1)}, s32[32,5]{0,1:T(8,128)}, u32[]{:S(2)}) copy-start(s32[32,5]{0,1:T(8,128)} %param.16) | copy-start | bytes 1924
  28.2 129.2 %all-gather.5.cloned.1.call-start = ((), (), s32[]{:S(2)}) async-start(), calls=%async_computation.5 | async-start | bytes 9437184 | tf_op jit(solution)/shard_map/all_gather | solution.py:90
  30.3 60.0 %all-to-all-start.2 = ((bf16[1,128,4,1024]{1,3,0,2:T(8,128)(2,1)}), bf16[1,128,4,1024]{1,3,0,2:T(8,128)(2,1)S(1)}, u32[]{:S(2)}, u32[]{:S(2)}) async-start(bf16[1,128,4,1024]{1,3,0,2:T(8,128)(2,1)} %bitcast.27), calls=%async_computation.2 | async-start | bytes 2097152 | tf_op jit(solution)/shard_map/all_to_all | solution.py:43
  33.8 184.3 %reduce-scatter.5.cloned.1.call-start = ((), (), s32[]{:S(2)}) async-start(), calls=%async_computation.6 | async-start | bytes 5242880 | tf_op jit(solution)/shard_map/reduce_scatter | solution.py:91
  81.4 2.6 copy-start.2
  93.0 6.6 %copy-start.3 = (bf16[5,4,128,256]{2,3,1,0:T(8,128)(2,1)S(1)}, bf16[5,4,128,256]{2,3,1,0:T(8,128)(2,1)}, u32[]{:S(2)}) copy-start(bf16[5,4,128,256]{2,3,1,0:T(8,128)(2,1)} %get-tuple-element.11) | copy-start | bytes 3932164
  166.8 0.7 copy-start.7
  166.8 51.3 %copy-start = (bf16[128,4096]{1,0:T(8,128)(2,1)S(1)}, bf16[128,4096]{1,0:T(8,128)(2,1)}, u32[]{:S(2)}) copy-start(bf16[128,4096]{1,0:T(8,128)(2,1)} %param.12) | copy-start | bytes 3145732
  166.8 52.9 %copy-start.5 = (f32[4096]{0:T(1024)S(1)}, f32[4096]{0:T(1024)}, u32[]{:S(2)}) copy-start(f32[4096]{0:T(1024)} %param.18) | copy-start | bytes 49156
  166.9 111.7 %all-gather.7.cloned.1.call-start = ((), (), s32[]{:S(2)}) async-start(), calls=%async_computation.7 | async-start | bytes 5898240 | tf_op jit(solution)/shard_map/all_gather | solution.py:114
  222.5 178.1 %reduce-scatter.7.cloned.1.call-start = ((), (), s32[]{:S(2)}) async-start(), calls=%async_computation.9 | async-start | bytes 5898240
  341.8 0.7 copy-start.8
  341.8 61.1 %copy-start.1 = (bf16[128,4096]{1,0:T(8,128)(2,1)S(1)}, bf16[128,4096]{1,0:T(8,128)(2,1)}, u32[]{:S(2)}) copy-start(bf16[128,4096]{1,0:T(8,128)(2,1)} %reduce-scatter.5.cloned.1.call-done) | copy-start | bytes 3145732
Sparse Core Ops, SparseCore 0:
  28.3 46.5 all-gather.8
  76.6 80.8 all-gather.4
  167.0 51.0 reduce-scatter.4
  222.6 55.9 all-gather.6
  341.9 58.5 reduce-scatter.6
where the time goes:
time: 413 us; the launch traced here: 412 us
  waiting for transfers between devices  261 us (63%)
  matrix products  62.7 us (15%)
  local copies, waits for them, and re-layouts  41.8 us (10%)
  other arithmetic  15.6 us (4%)
  between operations  13.4 us (3%)
  starting transfers between devices  9.19 us (2%)
  blocking collectives  8.1 us (2%)
    unnamed x6, waiting for transfers between devices  58.8 us
    all_gather x1, waiting for transfers between devices, local(): shard_piece = lax.all_gather(outgoing, 'ep', axis=1, tiled=True)  56.1 us
    all_gather x1, waiting for transfers between devices, local(): proj_full = lax.all_gather(out_proj, 'ep', axis=0, tiled=True)  52.8 us
    reduce_scatter x1, waiting for transfers between devices, local(): lax.psum_scatter(jnp.dot(attended, proj_full, preferred_element_type=jnp....  50.3 us
    all_gather x1, waiting for transfers between devices, local(): gathered = lax.all_gather(key_value[None], 'ep', axis=0, tiled=True)  38.7 us
    unnamed x25, local copies, waits for them, and re-layouts  29.7 us
    dot_general x1, matrix products, local(): jnp.einsum('wnf,wfd->wnd', activated, expert_down, preferred_element_type...  25.4 us
    dot_general x1, matrix products, local(): jnp.einsum('wnd,wfd->wnf', shard_piece, expert_gate, preferred_element_ty...  16.7 us
  transfers between devices with their start and end apart: 7, of which 6 were waited for; matrix products, arithmetic and copies ran while one was open for 8% of the time, Pallas kernels for 0%

commit v1 on v0

--- a/solution.py
+++ b/solution.py
@@ -87,7 +87,12 @@
     )
     attended = (summed / jnp.transpose(totals, (0, 3, 1, 2))[..., None]).astype(jnp.bfloat16)
     attended = attended.reshape(sp_count * tokens, query_width)
-    proj_full = lax.all_gather(out_proj, "ep", axis=0, tiled=True)
+    ring = [out_proj]
+    for hop in range(7):
+        ring.append(lax.ppermute(ring[-1], "ep", [(dev, (dev + 1) % 8) for dev in range(8)]))
+    proj_full = jnp.roll(
+        jnp.concatenate(ring[::-1], axis=0), (lax.axis_index("ep") + 1) * ring[0].shape[0], axis=0
+    )
     projected = lax.psum_scatter(
         jnp.dot(attended, proj_full, preferred_element_type=jnp.float32).astype(jnp.bfloat16),
         "sp",

time: 413 us -> 464 us (1.12)
  local copies, waits for them, and re-layouts: 41.8 us -> 69.7 us
  waiting for transfers between devices: 261 us -> 279 us
  blocking collectives: 8.1 us -> 0 us
  other arithmetic: 15.6 us -> 21.5 us
    ppermute x0 -> x7, waiting for transfers between devices: none -> 85.7 us  [local(): lax.ppermute(ring[-1], 'ep', [(dev, (dev + 1) % 8) for dev in range(8)])]
    all_gather x1 -> x0, waiting for transfers between devices: 52.8 us -> none  [local(): proj_full = lax.all_gather(out_proj, 'ep', axis=0, tiled=True)]
    unnamed x25 -> x50, local copies, waits for them, and re-layouts: 29.7 us -> 53.3 us
    all_gather x1, waiting for transfers between devices: 38.7 us -> 21.1 us  [local(): gathered = lax.all_gather(key_value[None], 'ep', axis=0, tiled=True)]
    all_to_all x1 -> x0, blocking collectives: 8.1 us -> none  [local(): lax.all_to_all(value_send, 'sp', split_axis=2, concat_axis=0, tiled=True)]
    all_to_all x0 -> x1, waiting for transfers between devices: none -> 7.06 us  [local(): lax.all_to_all(value_send, 'sp', split_axis=2, concat_axis=0, tiled=True)]
    unnamed x6 -> x5, waiting for transfers between devices: 58.8 us -> 58.1 us
  transfers between devices with their start and end apart: 7 -> 14, of which waited for: 6 -> 11; matrix products, arithmetic and copies ran while one was open for 8% -> 12% of each run, Pallas kernels for 0% -> 0%
where the time goes in v1:
time: 464 us; the launch traced here: 460 us
  waiting for transfers between devices  279 us (60%)
  local copies, waits for them, and re-layouts  69.7 us (15%)
  matrix products  62.9 us (14%)
  other arithmetic  21.5 us (5%)
  between operations  13.6 us (3%)
  starting transfers between devices  13.5 us (3%)
    ppermute x7, waiting for transfers between devices, local(): lax.ppermute(ring[-1], 'ep', [(dev, (dev + 1) % 8) for dev in range(8)])  85.7 us
    unnamed x5, waiting for transfers between devices  58.1 us
    all_gather x1, waiting for transfers between devices, local(): shard_piece = lax.all_gather(outgoing, 'ep', axis=1, tiled=True)  56.1 us
    unnamed x50, local copies, waits for them, and re-layouts  53.3 us
    reduce_scatter x1, waiting for transfers between devices, local(): lax.psum_scatter(jnp.dot(attended, proj_full, preferred_element_type=jnp....  50.6 us
    dot_general x1, matrix products, local(): jnp.einsum('wnf,wfd->wnd', activated, expert_down, preferred_element_type...  25.6 us
    all_gather x1, waiting for transfers between devices, local(): gathered = lax.all_gather(key_value[None], 'ep', axis=0, tiled=True)  21.1 us
    dot_general x1, matrix products, local(): jnp.einsum('wnd,wfd->wnf', shard_piece, expert_gate, preferred_element_ty...  16.7 us
  transfers between devices with their start and end apart: 14, of which 11 were waited for; matrix products, arithmetic and copies ran while one was open for 12% of the time, Pallas kernels for 0%

profile of v1, /device:TPU:0, one launch (start us, length us, event | category | flops | bytes accessed | tf_op | source)
XLA Modules:
  0.0 459.9 jit_solution(6874643450508324852)
XLA Ops:
  7.0 16.7 %collective-permute-done = bf16[128,4096]{1,0:T(8,128)(2,1)S(1)} collective-permute-done((bf16[128,4096]{1,0:T(8,128)(2,1)}, bf16[128,4096]{1,0:T(8,128)(2,1)S(1)}, u32[]{:S(2)}, u32[]{:S(2)}) %collective-permute-start) | collective-permute-done | bytes 1048608 | tf_op jit(solution)/shard_map/ppermute | solution.py:92
  23.7 16.0 %collective-permute-done.1 = bf16[128,4096]{1,0:T(8,128)(2,1)S(1)} collective-permute-done((bf16[128,4096]{1,0:T(8,128)(2,1)S(1)}, bf16[128,4096]{1,0:T(8,128)(2,1)S(1)}, u32[]{:S(2)}, u32[]{:S(2)}) %collective-permute-start.1) | collective-permute-done | bytes 1048608 | tf_op jit(solution)/shard_map/ppermute | solution.py:92
  39.8 16.0 %collective-permute-done.2 = bf16[128,4096]{1,0:T(8,128)(2,1)S(1)} collective-permute-done((bf16[128,4096]{1,0:T(8,128)(2,1)S(1)}, bf16[128,4096]{1,0:T(8,128)(2,1)S(1)}, u32[]{:S(2)}, u32[]{:S(2)}) %collective-permute-start.2) | collective-permute-done | bytes 1048608 | tf_op jit(solution)/shard_map/ppermute | solution.py:92
  56.8 16.0 %collective-permute-done.3 = bf16[128,4096]{1,0:T(8,128)(2,1)S(1)} collective-permute-done((bf16[128,4096]{1,0:T(8,128)(2,1)S(1)}, bf16[128,4096]{1,0:T(8,128)(2,1)S(1)}, u32[]{:S(2)}, u32[]{:S(2)}) %collective-permute-start.3) | collective-permute-done | bytes 1048608 | tf_op jit(solution)/shard_map/ppermute | solution.py:92
  73.8 16.0 %collective-permute-done.4 = bf16[128,4096]{1,0:T(8,128)(2,1)S(1)} collective-permute-done((bf16[128,4096]{1,0:T(8,128)(2,1)S(1)}, bf16[128,4096]{1,0:T(8,128)(2,1)S(1)}, u32[]{:S(2)}, u32[]{:S(2)}) %collective-permute-start.4) | collective-permute-done | bytes 1048608 | tf_op jit(solution)/shard_map/ppermute | solution.py:92
  91.8 4.2 all-to-all-start
  101.1 4.9 %collective-permute-done.5 = bf16[128,4096]{1,0:T(8,128)(2,1)} collective-permute-done((bf16[128,4096]{1,0:T(8,128)(2,1)S(1)}, bf16[128,4096]{1,0:T(8,128)(2,1)}, u32[]{:S(2)}, u32[]{:S(2)}) %collective-permute-start.5) | collective-permute-done | bytes 1048608 | tf_op jit(solution)/shard_map/ppermute | solution.py:92
  106.2 4.2 all-to-all-start.1
  111.4 7.1 %all-to-all-done.1 = bf16[1,128,4,256]{1,3,0,2:T(8,128)(2,1)} async-done(((bf16[1,128,4,256]{1,3,0,2:T(8,128)(2,1)}), bf16[1,128,4,256]{1,3,0,2:T(8,128)(2,1)}, u32[]{:S(2)}, u32[]{:S(2)}) %all-to-all-start.1) | async-done | bytes 262176 | tf_op jit(solution)/shard_map/all_to_all | solution.py:45
  118.4 3.5 all-to-all-start.2
  150.5 21.1 %all-gather.6.cloned.1.call-done = bf16[32,128,512]{2,1,0:T(8,128)(2,1)} async-done(((bf16[4,128,512]{2,1,0:T(8,128)(2,1)}), bf16[32,128,512]{2,1,0:T(8,128)(2,1)}) %all-gather.6.cloned.1.call-update) | async-done | bytes 4194320 | tf_op jit(solution)/shard_map/all_gather | solution.py:55
  171.6 6.5 %copy.48 = bf16[32,128,512]{1,2,0:T(8,128)(2,1)} copy(bf16[32,128,512]{2,1,0:T(8,128)(2,1)} %all-gather.6.cloned.1.call-done) | data formatting | bytes 8388608 | tf_op jit(solution)/shard_map/all_gather | solution.py:55
  187.5 3.1 fusion.36
  193.2 6.5 %fusion.3 = (f32[4,2,4,128]{3,2,1,0:T(4,128)S(1)}, bf16[4,2,4,128,5,128]{3,5,2,4,1,0:T(8,128)(2,1)}) fusion(f32[4,2,5,128,128,4]{4,3,5,2,1,0:T(8,128)S(1)} %get-tuple-element.14, f32[4,2,4,128]{3,2,1,0:T(4,128)S(1)} %get-tuple-element.13, pred[4,128,5,128]{1,3,2,0:T(8,128)(4,1)} %broadcast_and_fusion), kind=kLoop, calls=%fused_computation.5 | loop fusion | flops 15724544 | bytes 16089088 | tf_op jit(solution)/shard_map/reduce_sum | solution.py:83
  199.8 3.5 fusion.12
  204.8 9.5 %fusion.5 = bf16[512,4096]{1,0:T(8,128)(2,1)} fusion(bf16[512,1024]{1,0:T(8,128)(2,1)S(1)} %reshape.110, bf16[2048,4096]{1,0:T(8,128)(2,1)} %constant_dynamic-update-slice_fusion, s32[]{:T(128)S(6)} %select_n.109), kind=kOutput, calls=%fused_computation.8 | convolution fusion | flops 4297064448 | bytes 13631492 | tf_op jit(solution)/shard_map/dot_general | solution.py:97
  215.2 50.6 %reduce-scatter.5.cloned.1.call-done = bf16[128,4096]{1,0:T(8,128)(2,1)} async-done(((bf16[512,4096]{1,0:T(8,128)(2,1)}), bf16[128,4096]{1,0:T(8,128)(2,1)}) %reduce-scatter.5.cloned.1.call-update) | async-done | bytes 1048592 | tf_op jit(solution)/shard_map/reduce_scatter | solution.py:96
  267.5 2.7 convolution_convert_fusion.1
  270.3 56.1 %all-gather.4.cloned.1.call-done = bf16[2,320,4096]{2,1,0:T(8,128)(2,1)} async-done(((bf16[2,40,4096]{2,1,0:T(8,128)(2,1)}), bf16[2,320,4096]{2,1,0:T(8,128)(2,1)}) %all-gather.4.cloned.1.call-update) | async-done | bytes 5242896 | tf_op jit(solution)/shard_map/all_gather | solution.py:119
  326.4 16.7 %fusion.37 = f32[2,320,896]{2,1,0:T(8,128)} fusion(bf16[2,320,4096]{2,1,0:T(8,128)(2,1)} %all-gather.4.cloned.1.call-done, bf16[2,896,4096]{2,1,0:T(8,128)(2,1)} %param.21), kind=kOutput, calls=%fused_computation.81 | convolution fusion | flops 4697620480 | bytes 22216704 | tf_op jit(solution)/shard_map/wnd,wfd->wnf/dot_general | solution.py:120
  343.1 25.6 %convolution_convert_fusion = bf16[2,320,4096]{2,1,0:T(8,128)(2,1)} fusion(bf16[2,896,4096]{2,1,0:T(8,128)(2,1)} %param.23, f32[2,320,896]{2,1,0:T(8,128)} %fusion.37, bf16[2,320,4096]{2,1,0:T(8,128)(2,1)} %all-gather.4.cloned.1.call-done, bf16[2,896,4096]{2,1,0:T(8,128)(2,1)} %param.22), kind=kOutput, calls=%fused_computation.7 | convolution fusion | flops 9401303040 | bytes 42139648 | tf_op jit(solution)/shard_map/wnf,wfd->wnd/dot_general | solution.py:125
  368.7 10.4 %copy.68 = bf16[2,320,4096]{2,0,1:T(2,128)(2,1)} copy(bf16[2,320,4096]{2,1,0:T(8,128)(2,1)} %convolution_convert_fusion) | data formatting | bytes 10485760
  379.0 10.7 %copy.71 = bf16[40,8,2,4096]{3,1,2,0:T(8,128)(2,1)} copy(bf16[40,8,2,4096]{3,2,1,0:T(2,128)(2,1)} %bitcast.115) | data formatting | bytes 10485760
  390.5 58.1 %reduce-scatter.7.cloned.1.call-done = bf16[40,8192]{1,0:T(8,128)(2,1)} async-done(((bf16[320,8192]{1,0:T(8,128)(2,1)}), bf16[40,8192]{1,0:T(8,128)(2,1)}) %reduce-scatter.7.cloned.1.call-update) | async-done | bytes 655376
  (93 shorter events, 60.5 us)
Async XLA Ops:
  6.5 17.2 %collective-permute-start = (bf16[128,4096]{1,0:T(8,128)(2,1)}, bf16[128,4096]{1,0:T(8,128)(2,1)S(1)}, u32[]{:S(2)}, u32[]{:S(2)}) collective-permute-start(bf16[128,4096]{1,0:T(8,128)(2,1)} %param.17), channel_id=1, source_target_pairs={{0,1},{1,2},{2,3},{3,4},{4,5},{5,6},{6,7},{7,0},{8,9},{9,10},{10,1... | collective-permute-start | bytes 3145736 | tf_op jit(solution)/shard_map/ppermute | solution.py:92
  23.7 16.0 %collective-permute-start.1 = (bf16[128,4096]{1,0:T(8,128)(2,1)S(1)}, bf16[128,4096]{1,0:T(8,128)(2,1)S(1)}, u32[]{:S(2)}, u32[]{:S(2)}) collective-permute-start(bf16[128,4096]{1,0:T(8,128)(2,1)S(1)} %collective-permute-done), channel_id=1, source_target_pairs={{0,1},{1,2},{2,3},{3,4},{4,5},{5,6},{6,7},{7,0},{8,9},{9,10},{10,1... | collective-permute-start | bytes 3145736 | tf_op jit(solution)/shard_map/ppermute | solution.py:92
  39.8 16.0 %collective-permute-start.2 = (bf16[128,4096]{1,0:T(8,128)(2,1)S(1)}, bf16[128,4096]{1,0:T(8,128)(2,1)S(1)}, u32[]{:S(2)}, u32[]{:S(2)}) collective-permute-start(bf16[128,4096]{1,0:T(8,128)(2,1)S(1)} %collective-permute-done.1), channel_id=1, source_target_pairs={{0,1},{1,2},{2,3},{3,4},{4,5},{5,6},{6,7},{7,0},{8,9},{9,10},{10,1... | collective-permute-start | bytes 3145736 | tf_op jit(solution)/shard_map/ppermute | solution.py:92
  56.8 16.0 %collective-permute-start.3 = (bf16[128,4096]{1,0:T(8,128)(2,1)S(1)}, bf16[128,4096]{1,0:T(8,128)(2,1)S(1)}, u32[]{:S(2)}, u32[]{:S(2)}) collective-permute-start(bf16[128,4096]{1,0:T(8,128)(2,1)S(1)} %collective-permute-done.2), channel_id=1, source_target_pairs={{0,1},{1,2},{2,3},{3,4},{4,5},{5,6},{6,7},{7,0},{8,9},{9,10},{10,1... | collective-permute-start | bytes 3145736 | tf_op jit(solution)/shard_map/ppermute | solution.py:92
  73.8 16.0 %collective-permute-start.4 = (bf16[128,4096]{1,0:T(8,128)(2,1)S(1)}, bf16[128,4096]{1,0:T(8,128)(2,1)S(1)}, u32[]{:S(2)}, u32[]{:S(2)}) collective-permute-start(bf16[128,4096]{1,0:T(8,128)(2,1)S(1)} %collective-permute-done.3), channel_id=1, source_target_pairs={{0,1},{1,2},{2,3},{3,4},{4,5},{5,6},{6,7},{7,0},{8,9},{9,10},{10,1... | collective-permute-start | bytes 3145736 | tf_op jit(solution)/shard_map/ppermute | solution.py:92
  89.9 28.6 %copy-start.7 = (bf16[128,4096]{1,0:T(8,128)(2,1)}, bf16[128,4096]{1,0:T(8,128)(2,1)S(1)}, u32[]{:S(2)}) copy-start(bf16[128,4096]{1,0:T(8,128)(2,1)S(1)} %collective-permute-done.4) | copy-start | bytes 3145732
  89.9 16.1 %collective-permute-start.5 = (bf16[128,4096]{1,0:T(8,128)(2,1)S(1)}, bf16[128,4096]{1,0:T(8,128)(2,1)}, u32[]{:S(2)}, u32[]{:S(2)}) collective-permute-start(bf16[128,4096]{1,0:T(8,128)(2,1)S(1)} %collective-permute-done.4), channel_id=1, source_target_pairs={{0,1},{1,2},{2,3},{3,4},{4,5},{5,6},{6,7},{7,0},{8,9},{9,10},{10,1... | collective-permute-start | bytes 3145736 | tf_op jit(solution)/shard_map/ppermute | solution.py:92
  91.8 14.3 %all-to-all-start = ((bf16[1,128,4,256]{1,3,0,2:T(8,128)(2,1)}), bf16[1,128,4,256]{1,3,0,2:T(8,128)(2,1)S(1)}, u32[]{:S(2)}, u32[]{:S(2)}) async-start(bf16[1,128,4,256]{1,3,0,2:T(8,128)(2,1)} %bitcast.128), calls=%async_computation | async-start | bytes 524288 | tf_op jit(solution)/shard_map/all_to_all | solution.py:44
  106.0 22.4 %collective-permute-start.6 = (bf16[128,4096]{1,0:T(8,128)(2,1)}, bf16[128,4096]{1,0:T(8,128)(2,1)}, u32[]{:S(2)}, u32[]{:S(2)}) collective-permute-start(bf16[128,4096]{1,0:T(8,128)(2,1)} %collective-permute-done.5), channel_id=1, source_target_pairs={{0,1},{1,2},{2,3},{3,4},{4,5},{5,6},{6,7},{7,0},{8,9},{9,10},{10,1... | collective-permute-start | bytes 3145736 | tf_op jit(solution)/shard_map/ppermute | solution.py:92
  106.2 12.3 %copy-start.9 = (bf16[1,128,4,256]{1,3,0,2:T(8,128)(2,1)}, bf16[1,128,4,256]{1,3,0,2:T(8,128)(2,1)S(1)}, u32[]{:S(2)}) copy-start(bf16[1,128,4,256]{1,3,0,2:T(8,128)(2,1)S(1)} %all-to-all-done) | copy-start | bytes 786436
  106.2 12.3 %all-to-all-start.1 = ((bf16[1,128,4,256]{1,3,0,2:T(8,128)(2,1)}), bf16[1,128,4,256]{1,3,0,2:T(8,128)(2,1)}, u32[]{:S(2)}, u32[]{:S(2)}) async-start(bf16[1,128,4,256]{1,3,0,2:T(8,128)(2,1)} %bitcast.129), calls=%async_computation.1 | async-start | bytes 524288 | tf_op jit(solution)/shard_map/all_to_all | solution.py:45
  118.4 72.2 %all-to-all-start.2 = ((bf16[1,128,4,1024]{1,3,0,2:T(8,128)(2,1)}), bf16[1,128,4,1024]{1,3,0,2:T(8,128)(2,1)S(1)}, u32[]{:S(2)}, u32[]{:S(2)}) async-start(bf16[1,128,4,1024]{1,3,0,2:T(8,128)(2,1)} %bitcast.123), calls=%async_computation.2 | async-start | bytes 2097152 | tf_op jit(solution)/shard_map/all_to_all | solution.py:43
  122.0 49.7 %all-gather.6.cloned.1.call-start = ((), (), s32[]{:S(2)}) async-start(), calls=%async_computation.7 | async-start | bytes 4718592 | tf_op jit(solution)/shard_map/all_gather | solution.py:55
  126.0 139.8 %reduce-scatter.5.cloned.1.call-start = ((), (), s32[]{:S(2)}) async-start(), calls=%async_computation.5 | async-start | bytes 5242880 | tf_op jit(solution)/shard_map/reduce_scatter | solution.py:96
  126.3 6.8 %copy-start.8 = (bf16[128,4096]{1,0:T(8,128)(2,1)S(1)}, bf16[128,4096]{1,0:T(8,128)(2,1)}, u32[]{:S(2)}) copy-start(bf16[128,4096]{1,0:T(8,128)(2,1)} %copy-done.7) | copy-start | bytes 3145732
  126.3 7.8 %copy-start.6 = (bf16[128,4096]{1,0:T(8,128)(2,1)S(1)}, bf16[128,4096]{1,0:T(8,128)(2,1)}, u32[]{:S(2)}) copy-start(bf16[128,4096]{1,0:T(8,128)(2,1)} %copy-done.5) | copy-start | bytes 3145732
  126.4 8.8 %copy-start.4 = (bf16[128,4096]{1,0:T(8,128)(2,1)S(1)}, bf16[128,4096]{1,0:T(8,128)(2,1)}, u32[]{:S(2)}) copy-start(bf16[128,4096]{1,0:T(8,128)(2,1)} %copy-done.3) | copy-start | bytes 3145732
  193.2 6.5 %copy-start.10 = (bf16[5,4,128,256]{2,3,1,0:T(8,128)(2,1)S(1)}, bf16[5,4,128,256]{2,3,1,0:T(8,128)(2,1)}, u32[]{:S(2)}) copy-start(bf16[5,4,128,256]{2,3,1,0:T(8,128)(2,1)} %get-tuple-element.11) | copy-start | bytes 3932164
  204.7 10.1 %copy-start.12 = (s32[128,2]{0,1:T(2,128)S(1)}, s32[128,2]{0,1:T(2,128)}, u32[]{:S(2)}) copy-start(s32[128,2]{0,1:T(2,128)} %param.19) | copy-start | bytes 3076
  204.8 61.1 %copy-start = (bf16[128,4096]{1,0:T(8,128)(2,1)S(1)}, bf16[128,4096]{1,0:T(8,128)(2,1)}, u32[]{:S(2)}) copy-start(bf16[128,4096]{1,0:T(8,128)(2,1)} %param.12) | copy-start | bytes 3145732
  214.3 53.2 %copy-start.11 = (f32[4096]{0:T(1024)S(1)}, f32[4096]{0:T(1024)}, u32[]{:S(2)}) copy-start(f32[4096]{0:T(1024)} %param.18) | copy-start | bytes 49156
  214.3 112.1 %all-gather.4.cloned.1.call-start = ((), (), s32[]{:S(2)}) async-start(), calls=%async_computation.6 | async-start | bytes 5898240 | tf_op jit(solution)/shard_map/all_gather | solution.py:119
  270.2 178.3 %reduce-scatter.7.cloned.1.call-start = ((), (), s32[]{:S(2)}) async-start(), calls=%async_computation.8 | async-start | bytes 5898240
  389.8 61.1 %copy-start.1 = (bf16[128,4096]{1,0:T(8,128)(2,1)S(1)}, bf16[128,4096]{1,0:T(8,128)(2,1)}, u32[]{:S(2)}) copy-start(bf16[128,4096]{1,0:T(8,128)(2,1)} %reduce-scatter.5.cloned.1.call-done) | copy-start | bytes 3145732
  (4 other events, 8.0 us)
Sparse Core Ops, SparseCore 0:
  126.1 45.4 all-gather.5
  214.4 51.3 reduce-scatter.4
  270.3 55.9 all-gather.3
  389.9 58.5 reduce-scatter.6
